TPU v7x, 512 devices: a whole 4x4x16 slice. The times are simulated.
512 devices in a mesh: dp: 64 (over y, z), mp: 8 (over x, core).
Axes of the slice: x: 4, y: 4, z: 16, core: 2. Of those that a mesh axis runs over, the one named last changes fastest.
Arguments:
- tokens_in: bfloat16 [8192, 8192], P('dp', 'mp'), may hold values from -6 to 6
- gate_pre: bfloat16 [8192, 28672], P('dp', 'mp'), may hold values from -8 to 8
- up_pre: bfloat16 [8192, 28672], P('dp', 'mp'), may hold values from -6 to 6
- hidden_grad: bfloat16 [8192, 28672], P('dp', 'mp'), may hold values from -160 to 160
- out_grad: bfloat16 [8192, 8192], P('dp', 'mp'), may hold values from -160 to 160
- proj_model: bfloat16 [8192, 128], P('mp'), may hold values from -0.0625 to 0.0625
- proj_hidden: bfloat16 [28672, 128], P('mp'), may hold values from -0.03125 to 0.03125
Outputs:
- whitened: float32 [64, 128, 64], P('dp', 'mp')
All inputs are finite; a program needn't handle non-finite values.
Results may differ from a plain program's by a relative error of at most 0.003.
Values sent between devices are 32-bit elements; how exact they have to be, the bound alone decides.
A program may use at most 64 MiB of HBM per device.

v0:
```python
import math

import jax
import jax.numpy as jnp
from jax import lax
from jax.sharding import PartitionSpec as P

RANK = 64
LEN = 128


highest = lax.Precision.HIGHEST


def partner_2(value, axis, apart):
    mask = 2**apart
    pairs = [(source, source ^ mask) for source in range(lax.axis_size(axis))]
    return lax.ppermute(value, axis, pairs)


def gradient_blocks(projected):
    columns_each = projected.shape[-1] // 4
    input_side = projected[..., :columns_each]
    output_side = projected[..., columns_each : 2 * columns_each]
    upward = projected[..., 2 * columns_each : 3 * columns_each]
    hidden_side = projected[..., 3 * columns_each :]
    up_block = jnp.einsum("elr,els->ers", input_side, upward, precision=highest)
    down_block = jnp.einsum("elr,els->ers", hidden_side, output_side, precision=highest)
    return jnp.concatenate([up_block, down_block], axis=1)


def gram_of(rows):
    flat_rows = rows.reshape(-1, rows.shape[-1])
    return jnp.dot(flat_rows.T, flat_rows, precision=highest, preferred_element_type=jnp.float32)


def shards(tokens_in, gate_pre, up_pre, hidden_grad, out_grad, proj_model, proj_hidden):
    gate_act = jax.nn.silu(gate_pre.astype(jnp.float32))
    up_grad = (hidden_grad.astype(jnp.float32) * gate_act).astype(jnp.bfloat16)
    hidden = (gate_act * up_pre.astype(jnp.float32)).astype(jnp.bfloat16)
    local_sums = jnp.concatenate(
        [
            jnp.dot(tokens_in, proj_model[:, :RANK], preferred_element_type=jnp.float32),
            jnp.dot(out_grad, proj_model[:, RANK:], preferred_element_type=jnp.float32),
            jnp.dot(up_grad, proj_hidden[:, :RANK], preferred_element_type=jnp.float32),
            jnp.dot(hidden, proj_hidden[:, RANK:], preferred_element_type=jnp.float32),
        ],
        axis=1,
    )
    local_examples = tokens_in.shape[0] // LEN
    shaped = local_sums.reshape(local_examples, LEN, 4 * RANK)
    model_shards = lax.axis_size("mp")
    rows_each = 2 * RANK // model_shards
    summed = lax.psum(shaped, "mp")
    blocks = gradient_blocks(summed)
    mine = lax.dynamic_slice_in_dim(blocks, lax.axis_index("mp") * rows_each, rows_each, 1)
    group_gram = gram_of(blocks)
    flat_mine = mine.reshape(local_examples * rows_each, RANK)
    lower = jnp.linalg.cholesky(group_gram)
    for level in range(lax.axis_size("dp").bit_length() - 1):
        partner = partner_2(lower, "dp", level)
        combined = jnp.dot(
            lower, lower.T, precision=highest, preferred_element_type=jnp.float32
        ) + jnp.dot(partner, partner.T, precision=highest, preferred_element_type=jnp.float32)
        lower = jnp.linalg.cholesky(combined)
    solved = jax.scipy.linalg.solve_triangular(lower, flat_mine.T, lower=True)
    factor = math.sqrt(local_examples * lax.axis_size("dp") * 2 * RANK)
    return (solved.T * factor).reshape(local_examples, rows_each, RANK)


def solution(mesh):
    in_specs = (
        P("dp", "mp"),
        P("dp", "mp"),
        P("dp", "mp"),
        P("dp", "mp"),
        P("dp", "mp"),
        P("mp", None),
        P("mp", None),
    )
    out_specs = P("dp", "mp", None)
    return jax.shard_map(shards, mesh=mesh, in_specs=in_specs, out_specs=out_specs, check_vma=False)
```

profile of v0, /device:TPU:8, one launch (start us, length us, event | category | flops | bytes accessed | tf_op | source)
XLA Modules:
  0.0 209.8 jit_solution(459969425136288152)
XLA Ops:
  6.6 2.7 %fusion.4 = f32[128,64]{0,1:T(8,128)S(1)} fusion(bf16[128,3584]{1,0:T(8,128)(2,1)} %param.11, bf16[3584,128]{1,0:T(8,128)(2,1)} %param.14, bf16[128,3584]{1,0:T(8,128)(2,1)} %param.9), kind=kOutput, calls=%fused_computation.17 | convolution fusion | flops 62390272 | bytes 2785280 | tf_op jit(solution)/shard_map/dot_general | solution.py:45
  9.3 1.0 fusion.5
  10.3 0.2 fusion.10
  10.6 0.4 fusion.8
  11.0 0.7 maximum_bitcast_fusion
  11.7 79.8 %all-reduce.2.cloned.1.call-done = f32[1,128,256]{1,2,0:T(8,128)} async-done(((f32[1,128,256]{1,2,0:T(8,128)}), f32[1,128,256]{1,2,0:T(8,128)}) %all-reduce.2.cloned.1.call-update) | async-done | bytes 131088 | tf_op jit(solution)/shard_map/psum | solution.py:54
  91.5 1.0 convolution_bitcast_fusion
  92.5 1.0 convolution_bitcast_fusion.1
  93.4 0.3 fusion.15
  93.8 5.8 %cholesky.119 = f32[64,64]{1,0:T(8,128)S(1)} custom-call(f32[64,64]{1,0:T(8,128)S(1)} %fusion.23), custom_call_target="Cholesky" | custom-call | tf_op jit(solution)/shard_map/jit(cholesky)/cholesky | solution.py:59
  99.7 0.6 compare_reduce_fusion.6
  100.3 0.7 select_select_fusion.6
  101.0 3.5 %collective-permute-start = (f32[64,64]{1,0:T(8,128)S(1)}, f32[64,64]{1,0:T(8,128)S(1)}, u32[]{:S(2)}, u32[]{:S(2)}) collective-permute-start(f32[64,64]{1,0:T(8,128)S(1)} %select_select_fusion.6), channel_id=1, source_target_pairs={{0,8},{8,0},{16,24},{24,16},{32,40},{40,32},{48,56},{56,48},{64,72... | collective-permute-start | bytes 49160 | tf_op jit(solution)/shard_map/ppermute | solution.py:18
  104.6 2.1 %collective-permute-done = f32[64,64]{1,0:T(8,128)S(1)} collective-permute-done((f32[64,64]{1,0:T(8,128)S(1)}, f32[64,64]{1,0:T(8,128)S(1)}, u32[]{:S(2)}, u32[]{:S(2)}) %collective-permute-start) | collective-permute-done | bytes 16416 | tf_op jit(solution)/shard_map/ppermute | solution.py:18
  106.8 0.2 convolution_add_fusion.5
  107.1 5.8 %cholesky.130 = f32[64,64]{1,0:T(8,128)S(1)} custom-call(f32[64,64]{1,0:T(8,128)S(1)} %fusion.22), custom_call_target="Cholesky" | custom-call | tf_op jit(solution)/shard_map/jit(cholesky)/cholesky | solution.py:65
  113.0 0.6 compare_reduce_fusion.5
  113.6 0.7 select_select_fusion.5
  114.3 4.5 %collective-permute-start.1 = (f32[64,64]{1,0:T(8,128)S(1)}, f32[64,64]{1,0:T(8,128)S(1)}, u32[]{:S(2)}, u32[]{:S(2)}) collective-permute-start(f32[64,64]{1,0:T(8,128)S(1)} %select_select_fusion.5), channel_id=1, source_target_pairs={{0,16},{8,24},{16,0},{24,8},{32,48},{40,56},{48,32},{56,40},{64,80... | collective-permute-start | bytes 49160 | tf_op jit(solution)/shard_map/ppermute | solution.py:18
  118.9 2.1 collective-permute-done.1
  121.0 0.2 convolution_add_fusion.4
  121.2 5.8 %cholesky.141 = f32[64,64]{1,0:T(8,128)S(1)} custom-call(f32[64,64]{1,0:T(8,128)S(1)} %fusion.21), custom_call_target="Cholesky" | custom-call | tf_op jit(solution)/shard_map/jit(cholesky)/cholesky | solution.py:65
  127.1 0.6 compare_reduce_fusion.4
  127.8 0.7 select_select_fusion.4
  128.4 7.6 %collective-permute-start.2 = (f32[64,64]{1,0:T(8,128)S(1)}, f32[64,64]{1,0:T(8,128)S(1)}, u32[]{:S(2)}, u32[]{:S(2)}) collective-permute-start(f32[64,64]{1,0:T(8,128)S(1)} %select_select_fusion.4), channel_id=1, source_target_pairs={{0,32},{8,40},{16,48},{24,56},{32,0},{40,8},{48,16},{56,24},{64,96... | collective-permute-start | bytes 49160 | tf_op jit(solution)/shard_map/ppermute | solution.py:18
  136.3 1.9 collective-permute-done.2
  138.2 0.2 convolution_add_fusion.3
  138.4 5.8 %cholesky.152 = f32[64,64]{1,0:T(8,128)S(1)} custom-call(f32[64,64]{1,0:T(8,128)S(1)} %fusion.20), custom_call_target="Cholesky" | custom-call | tf_op jit(solution)/shard_map/jit(cholesky)/cholesky | solution.py:65
  144.3 0.6 compare_reduce_fusion.3
  145.0 0.7 select_select_fusion.3
  145.6 14.1 %collective-permute-start.3 = (f32[64,64]{1,0:T(8,128)S(1)}, f32[64,64]{1,0:T(8,128)S(1)}, u32[]{:S(2)}, u32[]{:S(2)}) collective-permute-start(f32[64,64]{1,0:T(8,128)S(1)} %select_select_fusion.3), channel_id=1, source_target_pairs={{0,64},{8,72},{16,80},{24,88},{32,96},{40,104},{48,112},{56,120},{... | collective-permute-start | bytes 49160 | tf_op jit(solution)/shard_map/ppermute | solution.py:18
  159.9 1.7 collective-permute-done.3
  161.6 0.2 convolution_add_fusion.2
  161.9 5.8 %cholesky.163 = f32[64,64]{1,0:T(8,128)S(1)} custom-call(f32[64,64]{1,0:T(8,128)S(1)} %fusion.19), custom_call_target="Cholesky" | custom-call | tf_op jit(solution)/shard_map/jit(cholesky)/cholesky | solution.py:65
  167.8 0.6 compare_reduce_fusion.2
  168.4 0.7 select_select_fusion.2
  169.1 2.4 %collective-permute-start.4 = (f32[64,64]{1,0:T(8,128)S(1)}, f32[64,64]{1,0:T(8,128)S(1)}, u32[]{:S(2)}, u32[]{:S(2)}) collective-permute-start(f32[64,64]{1,0:T(8,128)S(1)} %select_select_fusion.2), channel_id=1, source_target_pairs={{0,128},{8,136},{16,144},{24,152},{32,160},{40,168},{48,176},{56,1... | collective-permute-start | bytes 49160 | tf_op jit(solution)/shard_map/ppermute | solution.py:18
  171.7 3.2 %collective-permute-done.4 = f32[64,64]{1,0:T(8,128)S(1)} collective-permute-done((f32[64,64]{1,0:T(8,128)S(1)}, f32[64,64]{1,0:T(8,128)S(1)}, u32[]{:S(2)}, u32[]{:S(2)}) %collective-permute-start.4) | collective-permute-done | bytes 16416 | tf_op jit(solution)/shard_map/ppermute | solution.py:18
  175.2 5.8 %cholesky.174 = f32[64,64]{1,0:T(8,128)S(1)} custom-call(f32[64,64]{1,0:T(8,128)S(1)} %fusion.18), custom_call_target="Cholesky" | custom-call | tf_op jit(solution)/shard_map/jit(cholesky)/cholesky | solution.py:65
  181.1 0.6 compare_reduce_fusion.1
  181.7 0.7 select_select_fusion.1
  182.4 4.0 %collective-permute-start.5 = (f32[64,64]{1,0:T(8,128)S(1)}, f32[64,64]{1,0:T(8,128)S(1)}, u32[]{:S(2)}, u32[]{:S(2)}) collective-permute-start(f32[64,64]{1,0:T(8,128)S(1)} %select_select_fusion.1), channel_id=1, source_target_pairs={{0,256},{8,264},{16,272},{24,280},{32,288},{40,296},{48,304},{56,3... | collective-permute-start | bytes 49160 | tf_op jit(solution)/shard_map/ppermute | solution.py:18
  186.6 3.1 %collective-permute-done.5 = f32[64,64]{1,0:T(8,128)S(1)} collective-permute-done((f32[64,64]{1,0:T(8,128)S(1)}, f32[64,64]{1,0:T(8,128)S(1)}, u32[]{:S(2)}, u32[]{:S(2)}) %collective-permute-start.5) | collective-permute-done | bytes 16416 | tf_op jit(solution)/shard_map/ppermute | solution.py:18
  190.0 5.8 %cholesky.185 = f32[64,64]{1,0:T(8,128)S(1)} custom-call(f32[64,64]{1,0:T(8,128)S(1)} %fusion.17), custom_call_target="Cholesky" | custom-call | tf_op jit(solution)/shard_map/jit(cholesky)/cholesky | solution.py:65
  195.9 0.6 compare_reduce_fusion
  196.5 0.7 fusion.12
  197.2 4.9 %custom-call.6 = f32[1,64,64]{1,2,0:T(8,128)S(1)} custom-call(f32[1,64,64]{2,1,0:T(8,128)S(1)} %fusion.12), custom_call_target="InvertDiagBlocksLowerTriangular" | custom-call | tf_op jit(solution)/shard_map/jit(_solve_triangular)/triangular_solve | solution.py:66
  202.1 0.9 fusion.3
  (43 shorter events, 2.3 us)
Async XLA Ops:
  6.5 3.8 %copy-start = (bf16[128,1024]{1,0:T(8,128)(2,1)S(1)}, bf16[128,1024]{1,0:T(8,128)(2,1)}, u32[]{:S(2)}) copy-start(bf16[128,1024]{1,0:T(8,128)(2,1)} %param.8) | copy-start | bytes 786436
  6.5 2.7 %copy-start.4 = (bf16[3584,128]{1,0:T(8,128)(2,1)S(1)}, bf16[3584,128]{1,0:T(8,128)(2,1)}, u32[]{:S(2)}) copy-start(bf16[3584,128]{1,0:T(8,128)(2,1)} %param.14) | copy-start | bytes 2752516
  6.5 2.7 %copy-start.5 = (bf16[128,3584]{1,0:T(8,128)(2,1)S(1)}, bf16[128,3584]{1,0:T(8,128)(2,1)}, u32[]{:S(2)}) copy-start(bf16[128,3584]{1,0:T(8,128)(2,1)} %param.9) | copy-start | bytes 2752516
  6.5 2.7 %copy-start.3 = (bf16[128,3584]{1,0:T(8,128)(2,1)S(1)}, bf16[128,3584]{1,0:T(8,128)(2,1)}, u32[]{:S(2)}) copy-start(bf16[128,3584]{1,0:T(8,128)(2,1)} %param.10) | copy-start | bytes 2752516
  6.5 85.0 %all-reduce.2.cloned.1.call-start = ((), (), s32[]{:S(2)}) async-start(), calls=%async_computation | async-start | bytes 262144 | tf_op jit(solution)/shard_map/psum | solution.py:54
  9.3 1.0 copy-start.1
  9.3 1.3 copy-start.2
  101.0 5.8 %collective-permute-start = (f32[64,64]{1,0:T(8,128)S(1)}, f32[64,64]{1,0:T(8,128)S(1)}, u32[]{:S(2)}, u32[]{:S(2)}) collective-permute-start(f32[64,64]{1,0:T(8,128)S(1)} %select_select_fusion.6), channel_id=1, source_target_pairs={{0,8},{8,0},{16,24},{24,16},{32,40},{40,32},{48,56},{56,48},{64,72... | collective-permute-start | bytes 49160 | tf_op jit(solution)/shard_map/ppermute | solution.py:18
  114.3 6.7 %collective-permute-start.1 = (f32[64,64]{1,0:T(8,128)S(1)}, f32[64,64]{1,0:T(8,128)S(1)}, u32[]{:S(2)}, u32[]{:S(2)}) collective-permute-start(f32[64,64]{1,0:T(8,128)S(1)} %select_select_fusion.5), channel_id=1, source_target_pairs={{0,16},{8,24},{16,0},{24,8},{32,48},{40,56},{48,32},{56,40},{64,80... | collective-permute-start | bytes 49160 | tf_op jit(solution)/shard_map/ppermute | solution.py:18
  128.4 9.7 %collective-permute-start.2 = (f32[64,64]{1,0:T(8,128)S(1)}, f32[64,64]{1,0:T(8,128)S(1)}, u32[]{:S(2)}, u32[]{:S(2)}) collective-permute-start(f32[64,64]{1,0:T(8,128)S(1)} %select_select_fusion.4), channel_id=1, source_target_pairs={{0,32},{8,40},{16,48},{24,56},{32,0},{40,8},{48,16},{56,24},{64,96... | collective-permute-start | bytes 49160 | tf_op jit(solution)/shard_map/ppermute | solution.py:18
  145.6 16.0 %collective-permute-start.3 = (f32[64,64]{1,0:T(8,128)S(1)}, f32[64,64]{1,0:T(8,128)S(1)}, u32[]{:S(2)}, u32[]{:S(2)}) collective-permute-start(f32[64,64]{1,0:T(8,128)S(1)} %select_select_fusion.3), channel_id=1, source_target_pairs={{0,64},{8,72},{16,80},{24,88},{32,96},{40,104},{48,112},{56,120},{... | collective-permute-start | bytes 49160 | tf_op jit(solution)/shard_map/ppermute | solution.py:18
  169.1 5.8 %collective-permute-start.4 = (f32[64,64]{1,0:T(8,128)S(1)}, f32[64,64]{1,0:T(8,128)S(1)}, u32[]{:S(2)}, u32[]{:S(2)}) collective-permute-start(f32[64,64]{1,0:T(8,128)S(1)} %select_select_fusion.2), channel_id=1, source_target_pairs={{0,128},{8,136},{16,144},{24,152},{32,160},{40,168},{48,176},{56,1... | collective-permute-start | bytes 49160 | tf_op jit(solution)/shard_map/ppermute | solution.py:18
  182.4 7.3 %collective-permute-start.5 = (f32[64,64]{1,0:T(8,128)S(1)}, f32[64,64]{1,0:T(8,128)S(1)}, u32[]{:S(2)}, u32[]{:S(2)}) collective-permute-start(f32[64,64]{1,0:T(8,128)S(1)} %select_select_fusion.1), channel_id=1, source_target_pairs={{0,256},{8,264},{16,272},{24,280},{32,288},{40,296},{48,304},{56,3... | collective-permute-start | bytes 49160 | tf_op jit(solution)/shard_map/ppermute | solution.py:18
Sparse Core Ops, SparseCore 0:
  11.8 79.6 all-reduce.1
where the time goes:
time: 210 us
  waiting for transfers between devices  93.9 us (45%)
  other arithmetic  55.8 us (27%)
  starting transfers between devices  36.1 us (17%)
  between operations  13.8 us (7%)
  matrix products  9.57 us (5%)
    psum x1, waiting for transfers between devices, shards(): summed = lax.psum(shaped, 'mp')  79.8 us
    another operation x18, other arithmetic, shards(): lower = jnp.linalg.cholesky(combined)  39.1 us
    ppermute x6, starting transfers between devices, partner_2(): return lax.ppermute(value, axis, pairs)  36.1 us
    ppermute x6, waiting for transfers between devices, partner_2(): return lax.ppermute(value, axis, pairs)  14.1 us
    another operation x3, other arithmetic, shards(): lower = jnp.linalg.cholesky(group_gram)  6.52 us
    another operation x2, other arithmetic, shards(): solved = jax.scipy.linalg.solve_triangular(lower, flat_mine.T, lower=True)  5.55 us
  transfers between devices with their start and end apart: 7, of which 7 were waited for; matrix products, arithmetic and copies ran while one was open for 1% of the time, Pallas kernels for 0%

commit v1 on v0

v1 whole, which is shorter than its diff:
```python
import functools
import math

import jax
import jax.numpy as jnp
from jax import lax
from jax.experimental import pallas as pl
from jax.experimental.pallas import tpu as pltpu
from jax.sharding import PartitionSpec as P

RANK = 64
LEN = 128
NY, NZ = 4, 16
NC = 2
CHUNK = 512
F32 = jnp.float32
BF16 = jnp.bfloat16
MESH = pl.DeviceIdType.MESH
NT = (((1,), (1,)), ((), ()))


def halves(value):
    high = value.astype(BF16)
    return high, (value - high.astype(F32)).astype(BF16)


def thirds(value):
    high = value.astype(BF16)
    rest = value - high.astype(F32)
    mid = rest.astype(BF16)
    return high, mid, (rest - mid.astype(F32)).astype(BF16)


def product_3(left, right):
    lh, ll = halves(left)
    rh, rl = halves(right)
    return lax.dot_general(
        jnp.concatenate([lh, lh, ll], axis=1),
        jnp.concatenate([rh, rl, rh], axis=1),
        NT,
        preferred_element_type=F32,
    )


def product_6(left, right):
    lh, lm, ll = thirds(left)
    rh, rm, rl = thirds(right)
    return lax.dot_general(
        jnp.concatenate([ll, lm, lh, lm, lh, lh], axis=1),
        jnp.concatenate([rh, rm, rl, rh, rm, rh], axis=1),
        NT,
        preferred_element_type=F32,
    )


def kernel(
    mp_size,
    tokens_hbm,
    gate_hbm,
    up_hbm,
    hidden_grad_hbm,
    out_grad_hbm,
    model_hbm,
    hidden_hbm,
    out_ref,
    tokens,
    gate,
    up,
    hidden_grad,
    out_grad,
    model,
    hidden,
    lhs,
    part,
    from_core,
    xbuf,
    sbuf,
    mbuf,
    packed,
    zbuf,
    fbuf,
    aug,
    rows_out,
    in_sem,
    chunk_sem,
    core_sem,
    x_sem,
    m_sem,
    z_sem,
    f_sem,
):
    nx = mp_size // NC
    dp = lax.axis_index("dp")
    mp = lax.axis_index("mp")
    y, z = dp // NZ, dp % NZ
    x, core = mp // NC, mp % NC
    chunks = gate.shape[0]

    first = [
        pltpu.make_async_copy(model_hbm, model, in_sem.at[0]),
        pltpu.make_async_copy(tokens_hbm, tokens, in_sem.at[1]),
        pltpu.make_async_copy(out_grad_hbm, out_grad, in_sem.at[2]),
    ]
    for copy in first:
        copy.start()
    later = []
    for i in range(chunks):
        span = pl.ds(i * CHUNK, CHUNK)
        group = [
            pltpu.make_async_copy(hidden_hbm.at[span, :], hidden.at[i], chunk_sem.at[i, 0]),
            pltpu.make_async_copy(gate_hbm.at[:, span], gate.at[i], chunk_sem.at[i, 1]),
            pltpu.make_async_copy(hidden_grad_hbm.at[:, span], hidden_grad.at[i], chunk_sem.at[i, 2]),
            pltpu.make_async_copy(up_hbm.at[:, span], up.at[i], chunk_sem.at[i, 3]),
        ]
        for copy in group:
            copy.start()
        later.append(group)

    barrier = pltpu.get_barrier_semaphore()
    plane = NY * mp_size

    def z_peer(apart):
        return (y * NZ + (z + apart) % NZ, mp)

    def plane_peer(apart):
        there = (y * mp_size + mp + apart) % plane
        return ((there // mp_size) * NZ + z, there % mp_size)

    def greet_z(apart, carry):
        pl.semaphore_signal(barrier, inc=1, device_id=z_peer(apart), device_id_type=MESH)
        return carry

    def greet_plane(apart, carry):
        pl.semaphore_signal(barrier, inc=1, device_id=plane_peer(apart), device_id_type=MESH)
        return carry

    lax.fori_loop(1, NZ, greet_z, 0)
    lax.fori_loop(1, plane, greet_plane, 0)

    for copy in first:
        copy.wait()
    from_model = jnp.dot(tokens[...], model[...], preferred_element_type=F32)
    from_model_out = jnp.dot(out_grad[...], model[...], preferred_element_type=F32)
    total = jnp.zeros((2 * LEN, 2 * RANK), F32)
    for i in range(chunks):
        for copy in later[i]:
            copy.wait()
        slot = i % 2
        for r in range(0, LEN, 32):
            block = pl.ds(r, 32)
            g = gate[i, block, :].astype(F32)
            half = 0.5 * g
            act = half + half * jnp.tanh(half)
            lhs[slot, block, :] = (hidden_grad[i, block, :].astype(F32) * act).astype(BF16)
            lhs[slot, pl.ds(LEN + r, 32), :] = (act * up[i, block, :].astype(F32)).astype(BF16)
        total = total + jnp.dot(lhs[slot], hidden[i], preferred_element_type=F32)
    lane = lax.broadcasted_iota(jnp.int32, (LEN, 2 * RANK), 1)
    low = lane < RANK
    part[0] = jnp.where(low, from_model, pltpu.roll(total[:LEN], RANK, 1))
    part[1] = jnp.where(low, pltpu.roll(from_model_out, RANK, 1), total[LEN:])

    pl.semaphore_wait(barrier, NZ - 1 + plane - 1)

    sibling = (dp, x * NC + 1 - core)
    swap = pltpu.make_async_remote_copy(
        part.at[1 - core], from_core, core_sem.at[0], core_sem.at[1], device_id=sibling, device_id_type=MESH
    )
    swap.start()
    swap.wait()
    xbuf[x] = part[core] + from_core[...]

    for apart in range(1, nx):
        pltpu.make_async_remote_copy(
            xbuf.at[x],
            xbuf.at[x],
            x_sem.at[0],
            x_sem.at[1],
            device_id=(dp, ((x + apart) % nx) * NC + core),
            device_id_type=MESH,
        ).start()
    all_x = pltpu.make_async_remote_copy(
        xbuf.at[pl.ds(0, nx - 1)],
        xbuf.at[pl.ds(0, nx - 1)],
        x_sem.at[0],
        x_sem.at[1],
        device_id=sibling,
        device_id_type=MESH,
    )
    all_x.wait_send()
    all_x.wait_recv()
    summed = xbuf[0]
    for i in range(1, nx):
        summed = summed + xbuf[i]

    turned = summed.T
    sbuf[...] = product_3(turned, turned)
    mine = pl.ds(pl.multiple_of((1 - core) * RANK, RANK), RANK)
    mbuf[core] = sbuf[mine, :]
    give = pltpu.make_async_remote_copy(
        mbuf.at[core], mbuf.at[core], m_sem.at[0], m_sem.at[1], device_id=sibling, device_id_type=MESH
    )
    give.start()
    give.wait()
    short_low = lax.broadcasted_iota(jnp.int32, (RANK, 2 * RANK), 1) < RANK
    stacked = jnp.where(short_low, mbuf[0], mbuf[1])

    gram = product_6(stacked, jnp.concatenate([stacked, stacked], axis=0))
    half_low = lax.broadcasted_iota(jnp.int32, (RANK // 2, 2 * RANK), 1) < RANK
    pairs = jnp.where(half_low, gram[: RANK // 2], gram[RANK // 2 :])
    size = packed.shape[1]
    for i in range(mp_size):
        packed[i] = pairs[i * size : (i + 1) * size]

    for apart in sorted(range(1, NZ), key=lambda d: -min(d, NZ - d)):
        pltpu.make_async_remote_copy(
            packed.at[mp], zbuf.at[z], z_sem.at[0], z_sem.at[1], device_id=z_peer(apart), device_id_type=MESH
        ).start()
    zbuf[z] = packed[mp]
    own = pltpu.roll(stacked, (RANK + 2 * RANK - mp * (2 * RANK // mp_size)) % (2 * RANK), 1)
    all_z = pltpu.make_async_remote_copy(
        zbuf.at[pl.ds(0, NZ - 1)],
        zbuf.at[pl.ds(0, NZ - 1)],
        z_sem.at[0],
        z_sem.at[1],
        device_id=sibling,
        device_id_type=MESH,
    )
    all_z.wait_send()
    all_z.wait_recv()
    slice_sum = zbuf[0]
    for i in range(1, NZ):
        slice_sum = slice_sum + zbuf[i]
    place = y * mp_size + mp
    fbuf[place] = slice_sum

    def send_plane(apart, carry):
        pltpu.make_async_remote_copy(
            fbuf.at[place], fbuf.at[place], f_sem.at[0], f_sem.at[1], device_id=plane_peer(apart), device_id_type=MESH
        ).start()
        return carry

    lax.fori_loop(1, plane, send_plane, 0)
    all_plane = pltpu.make_async_remote_copy(
        fbuf.at[pl.ds(0, plane - 1)],
        fbuf.at[pl.ds(0, plane - 1)],
        f_sem.at[0],
        f_sem.at[1],
        device_id=sibling,
        device_id_type=MESH,
    )
    all_plane.wait_send()
    all_plane.wait_recv()
    for i in range(mp_size):
        piece = fbuf[i]
        for j in range(1, NY):
            piece = piece + fbuf[j * mp_size + i]
        aug[i * size : (i + 1) * size, :] = piece
    folded = aug[...]
    whole = jnp.concatenate([folded, pltpu.roll(folded, RANK, 1)], axis=0)
    table = jnp.where(short_low, whole, own)

    tiles = [table[8 * i : 8 * i + 8] for i in range(RANK // 8)]
    for k in range(RANK):
        t, s = k // 8, k % 8
        row = jnp.broadcast_to(tiles[t][s : s + 1, :], (8, 2 * RANK))
        pivot = jnp.broadcast_to(row[:, k : k + 1], (8, 2 * RANK))
        rows_out[k : k + 1, :] = (row * lax.rsqrt(pivot))[:1]
        scaled = row / pivot
        for i in range(t, RANK // 8):
            column = jnp.broadcast_to(tiles[i][:, k : k + 1], (8, 2 * RANK))
            tiles[i] = tiles[i] - column * scaled
    factor = math.sqrt(NY * NZ * LEN)
    turned_out = rows_out[...].T
    out_ref[0] = turned_out[RANK : RANK + 2 * RANK // mp_size, :RANK] * factor


def shards(tokens_in, gate_pre, up_pre, hidden_grad, out_grad, proj_model, proj_hidden):
    mp_size = lax.axis_size("mp")
    length, width = tokens_in.shape
    units = gate_pre.shape[1]
    chunks = units // CHUNK
    ranks = 2 * RANK
    size = RANK * RANK // (mp_size * ranks)
    any_space = pl.BlockSpec(memory_space=pl.ANY)
    return pl.pallas_call(
        functools.partial(kernel, mp_size),
        out_shape=jax.ShapeDtypeStruct((1, ranks // mp_size, RANK), F32),
        in_specs=[any_space] * 7,
        out_specs=pl.BlockSpec(memory_space=pltpu.VMEM),
        scratch_shapes=[
            pltpu.VMEM((length, width), BF16),
            pltpu.VMEM((chunks, length, CHUNK), BF16),
            pltpu.VMEM((chunks, length, CHUNK), BF16),
            pltpu.VMEM((chunks, length, CHUNK), BF16),
            pltpu.VMEM((length, width), BF16),
            pltpu.VMEM((width, ranks), BF16),
            pltpu.VMEM((chunks, CHUNK, ranks), BF16),
            pltpu.VMEM((2, 2 * length, CHUNK), BF16),
            pltpu.VMEM((2, length, ranks), F32),
            pltpu.VMEM((length, ranks), F32),
            pltpu.VMEM((mp_size // NC, length, ranks), F32),
            pltpu.VMEM((ranks, ranks), F32),
            pltpu.VMEM((2, RANK, ranks), F32),
            pltpu.VMEM((mp_size, size, ranks), F32),
            pltpu.VMEM((NZ, size, ranks), F32),
            pltpu.VMEM((NY * mp_size, size, ranks), F32),
            pltpu.VMEM((RANK // 2, ranks), F32),
            pltpu.VMEM((ranks, ranks), F32),
            pltpu.SemaphoreType.DMA((3,)),
            pltpu.SemaphoreType.DMA((chunks, 4)),
            pltpu.SemaphoreType.DMA((2,)),
            pltpu.SemaphoreType.DMA((2,)),
            pltpu.SemaphoreType.DMA((2,)),
            pltpu.SemaphoreType.DMA((2,)),
            pltpu.SemaphoreType.DMA((2,)),
        ],
        compiler_params=pltpu.CompilerParams(collective_id=0, has_side_effects=True),
        name="whiten",
    )(tokens_in, gate_pre, up_pre, hidden_grad, out_grad, proj_model, proj_hidden)


def solution(mesh):
    in_specs = (
        P("dp", "mp"),
        P("dp", "mp"),
        P("dp", "mp"),
        P("dp", "mp"),
        P("dp", "mp"),
        P("mp", None),
        P("mp", None),
    )
    out_specs = P("dp", "mp", None)
    return jax.shard_map(shards, mesh=mesh, in_specs=in_specs, out_specs=out_specs, check_vma=False)
```

time: 210 us -> 47.4 us (0.23)
  the two profiles are of different devices: /device:TPU:8 before, /device:TPU:1 now
where the time goes in v1:
time: 47.4 us; the launch traced here: 47.3 us
  Pallas kernels  46 us (97%)
  local copies, waits for them, and re-layouts  1.3 us (3%)
    pallas_call x1, Pallas kernels, shards(): pl.pallas_call(functools.partial(kernel, mp_size), out_shape=jax.ShapeDty...  46 us
    unnamed x1, local copies, waits for them, and re-layouts  1.3 us

profile of v1, /device:TPU:1, one launch (start us, length us, event | category | flops | bytes accessed | tf_op | source)
XLA Modules:
  0.0 47.3 jit_solution(17903349753724403282)
XLA Ops:
  0.0 46.0 %whiten.1 = f32[1,16,64]{2,1,0:T(8,128)} custom-call(bf16[128,1024]{1,0:T(8,128)(2,1)} %tokens_hbm.1, bf16[128,3584]{1,0:T(8,128)(2,1)} %gate_hbm.1, bf16[128,3584]{1,0:T(8,128)(2,1)} %up_hbm.1, bf16[128,3584]{1,0:T(8,128)(2,1)} %hidden_grad_hbm.1, bf16[128,1024]{1,0:T(8,128)(2,1)} %out_grad_hbm.1, bf16[1024,128]{1,0:T(8,128)(2,1)} %model_hbm.1, ...), custom_call_target="tpu_custom_call" | custom-call | tf_op jit(solution)/shard_map/whiten/pallas_call | solution.py:285
  46.0 1.3 %copy.9 = f32[1,16,64]{2,1,0:T(8,128)} copy(f32[1,16,64]{2,1,0:T(8,128)} %whiten.1) | data formatting | bytes 8192

commit v2 on v1

--- a/solution.py
+++ b/solution.py
@@ -12,7 +12,7 @@
 LEN = 128
 NY, NZ = 4, 16
 NC = 2
-CHUNK = 512
+ROWS = 64
 F32 = jnp.float32
 BF16 = jnp.bfloat16
 MESH = pl.DeviceIdType.MESH
@@ -51,6 +51,31 @@
         NT,
         preferred_element_type=F32,
     )
+
+
+def eliminate(table, rows_out):
+    width = table.shape[1]
+    tiles = [table[i : i + 8] for i in range(0, RANK, 8)]
+    for t in range(RANK // 8):
+        columns = [
+            [jnp.broadcast_to(tile[:, 8 * t + j : 8 * t + j + 1], tile.shape) for tile in tiles[t:]] for j in range(8)
+        ]
+        rows = [jnp.broadcast_to(tiles[t][j : j + 1], (8, width)) for j in range(8)]
+        pivot = [[jnp.broadcast_to(columns[j][0][i : i + 1], (8, width)) for j in range(i + 1)] for i in range(8)]
+        scaled = []
+        for j in range(8):
+            inverse = 1.0 / pivot[j][j]
+            rows_out[8 * t + j : 8 * t + j + 1, :] = (rows[j] * lax.rsqrt(pivot[j][j]))[:1]
+            for m in range(j + 1, 8):
+                share = pivot[m][j] * inverse
+                rows[m] = rows[m] - share * rows[j]
+                for n in range(j + 1, m + 1):
+                    pivot[m][n] = pivot[m][n] - share * pivot[n][j]
+                columns[m] = [late - share * early for late, early in zip(columns[m], columns[j])]
+            scaled.append(rows[j] * inverse)
+        for i in range(t + 1, RANK // 8):
+            for j in range(8):
+                tiles[i] = tiles[i] - columns[j][i - t] * scaled[j]
 
 
 def kernel(
@@ -82,7 +107,7 @@
     aug,
     rows_out,
     in_sem,
-    chunk_sem,
+    block_sem,
     core_sem,
     x_sem,
     m_sem,
@@ -94,27 +119,27 @@
     mp = lax.axis_index("mp")
     y, z = dp // NZ, dp % NZ
     x, core = mp // NC, mp % NC
-    chunks = gate.shape[0]
-
-    first = [
-        pltpu.make_async_copy(model_hbm, model, in_sem.at[0]),
-        pltpu.make_async_copy(tokens_hbm, tokens, in_sem.at[1]),
-        pltpu.make_async_copy(out_grad_hbm, out_grad, in_sem.at[2]),
+
+    weights = pltpu.make_async_copy(hidden_hbm, hidden, in_sem.at[0])
+    last = [
+        pltpu.make_async_copy(model_hbm, model, in_sem.at[1]),
+        pltpu.make_async_copy(tokens_hbm, tokens, in_sem.at[2]),
+        pltpu.make_async_copy(out_grad_hbm, out_grad, in_sem.at[3]),
     ]
-    for copy in first:
-        copy.start()
-    later = []
-    for i in range(chunks):
-        span = pl.ds(i * CHUNK, CHUNK)
+    weights.start()
+    blocks = []
+    for i in range(LEN // ROWS):
+        span = pl.ds(i * ROWS, ROWS)
         group = [
-            pltpu.make_async_copy(hidden_hbm.at[span, :], hidden.at[i], chunk_sem.at[i, 0]),
-            pltpu.make_async_copy(gate_hbm.at[:, span], gate.at[i], chunk_sem.at[i, 1]),
-            pltpu.make_async_copy(hidden_grad_hbm.at[:, span], hidden_grad.at[i], chunk_sem.at[i, 2]),
-            pltpu.make_async_copy(up_hbm.at[:, span], up.at[i], chunk_sem.at[i, 3]),
+            pltpu.make_async_copy(gate_hbm.at[span, :], gate.at[span, :], block_sem.at[i, 0]),
+            pltpu.make_async_copy(hidden_grad_hbm.at[span, :], hidden_grad.at[span, :], block_sem.at[i, 1]),
+            pltpu.make_async_copy(up_hbm.at[span, :], up.at[span, :], block_sem.at[i, 2]),
         ]
         for copy in group:
             copy.start()
-        later.append(group)
+        blocks.append(group)
+    for copy in last:
+        copy.start()
 
     barrier = pltpu.get_barrier_semaphore()
     plane = NY * mp_size
@@ -137,27 +162,28 @@
     lax.fori_loop(1, NZ, greet_z, 0)
     lax.fori_loop(1, plane, greet_plane, 0)
 
-    for copy in first:
+    weights.wait()
+    upward, downward = [], []
+    for i, group in enumerate(blocks):
+        for copy in group:
+            copy.wait()
+        for r in range(i * ROWS, (i + 1) * ROWS, 32):
+            span = pl.ds(r, 32)
+            half = 0.5 * gate[span, :].astype(F32)
+            act = half + half * jnp.tanh(half)
+            lhs[0, span, :] = (hidden_grad[span, :].astype(F32) * act).astype(BF16)
+            lhs[1, span, :] = (act * up[span, :].astype(F32)).astype(BF16)
+        span = pl.ds(i * ROWS, ROWS)
+        upward.append(jnp.dot(lhs[0, span, :], hidden[...], preferred_element_type=F32))
+        downward.append(jnp.dot(lhs[1, span, :], hidden[...], preferred_element_type=F32))
+    for copy in last:
         copy.wait()
-    from_model = jnp.dot(tokens[...], model[...], preferred_element_type=F32)
-    from_model_out = jnp.dot(out_grad[...], model[...], preferred_element_type=F32)
-    total = jnp.zeros((2 * LEN, 2 * RANK), F32)
-    for i in range(chunks):
-        for copy in later[i]:
-            copy.wait()
-        slot = i % 2
-        for r in range(0, LEN, 32):
-            block = pl.ds(r, 32)
-            g = gate[i, block, :].astype(F32)
-            half = 0.5 * g
-            act = half + half * jnp.tanh(half)
-            lhs[slot, block, :] = (hidden_grad[i, block, :].astype(F32) * act).astype(BF16)
-            lhs[slot, pl.ds(LEN + r, 32), :] = (act * up[i, block, :].astype(F32)).astype(BF16)
-        total = total + jnp.dot(lhs[slot], hidden[i], preferred_element_type=F32)
+    inward = jnp.dot(tokens[...], model[...], preferred_element_type=F32)
+    outward = jnp.dot(out_grad[...], model[...], preferred_element_type=F32)
     lane = lax.broadcasted_iota(jnp.int32, (LEN, 2 * RANK), 1)
     low = lane < RANK
-    part[0] = jnp.where(low, from_model, pltpu.roll(total[:LEN], RANK, 1))
-    part[1] = jnp.where(low, pltpu.roll(from_model_out, RANK, 1), total[LEN:])
+    part[0] = jnp.where(low, inward, pltpu.roll(jnp.concatenate(upward, axis=0), RANK, 1))
+    part[1] = jnp.where(low, pltpu.roll(outward, RANK, 1), jnp.concatenate(downward, axis=0))
 
     pl.semaphore_wait(barrier, NZ - 1 + plane - 1)
 
@@ -259,16 +285,7 @@
     whole = jnp.concatenate([folded, pltpu.roll(folded, RANK, 1)], axis=0)
     table = jnp.where(short_low, whole, own)
 
-    tiles = [table[8 * i : 8 * i + 8] for i in range(RANK // 8)]
-    for k in range(RANK):
-        t, s = k // 8, k % 8
-        row = jnp.broadcast_to(tiles[t][s : s + 1, :], (8, 2 * RANK))
-        pivot = jnp.broadcast_to(row[:, k : k + 1], (8, 2 * RANK))
-        rows_out[k : k + 1, :] = (row * lax.rsqrt(pivot))[:1]
-        scaled = row / pivot
-        for i in range(t, RANK // 8):
-            column = jnp.broadcast_to(tiles[i][:, k : k + 1], (8, 2 * RANK))
-            tiles[i] = tiles[i] - column * scaled
+    eliminate(table, rows_out)
     factor = math.sqrt(NY * NZ * LEN)
     turned_out = rows_out[...].T
     out_ref[0] = turned_out[RANK : RANK + 2 * RANK // mp_size, :RANK] * factor
@@ -278,24 +295,23 @@
     mp_size = lax.axis_size("mp")
     length, width = tokens_in.shape
     units = gate_pre.shape[1]
-    chunks = units // CHUNK
     ranks = 2 * RANK
     size = RANK * RANK // (mp_size * ranks)
     any_space = pl.BlockSpec(memory_space=pl.ANY)
     return pl.pallas_call(
         functools.partial(kernel, mp_size),
-        out_shape=jax.ShapeDtypeStruct((1, ranks // mp_size, RANK), F32),
+        out_shape=pltpu.VMEM((1, ranks // mp_size, RANK), F32),
         in_specs=[any_space] * 7,
         out_specs=pl.BlockSpec(memory_space=pltpu.VMEM),
         scratch_shapes=[
             pltpu.VMEM((length, width), BF16),
-            pltpu.VMEM((chunks, length, CHUNK), BF16),
-            pltpu.VMEM((chunks, length, CHUNK), BF16),
-            pltpu.VMEM((chunks, length, CHUNK), BF16),
+            pltpu.VMEM((length, units), BF16),
+            pltpu.VMEM((length, units), BF16),
+            pltpu.VMEM((length, units), BF16),
             pltpu.VMEM((length, width), BF16),
             pltpu.VMEM((width, ranks), BF16),
-            pltpu.VMEM((chunks, CHUNK, ranks), BF16),
-            pltpu.VMEM((2, 2 * length, CHUNK), BF16),
+            pltpu.VMEM((units, ranks), BF16),
+            pltpu.VMEM((2, length, units), BF16),
             pltpu.VMEM((2, length, ranks), F32),
             pltpu.VMEM((length, ranks), F32),
             pltpu.VMEM((mp_size // NC, length, ranks), F32),
@@ -306,8 +322,8 @@
             pltpu.VMEM((NY * mp_size, size, ranks), F32),
             pltpu.VMEM((RANK // 2, ranks), F32),
             pltpu.VMEM((ranks, ranks), F32),
-            pltpu.SemaphoreType.DMA((3,)),
-            pltpu.SemaphoreType.DMA((chunks, 4)),
+            pltpu.SemaphoreType.DMA((4,)),
+            pltpu.SemaphoreType.DMA((LEN // ROWS, 3)),
             pltpu.SemaphoreType.DMA((2,)),
             pltpu.SemaphoreType.DMA((2,)),
             pltpu.SemaphoreType.DMA((2,)),

time: 47.4 us -> 39.3 us (0.83)
  Pallas kernels: 46 us -> 38.5 us
  local copies, waits for them, and re-layouts: 1.3 us -> 0.6 us
    pallas_call x1, Pallas kernels: 46 us -> 38.5 us  [shards(): pl.pallas_call(functools.partial(kernel, mp_size), out_shape=pltpu.VMEM((...]
    unnamed x1, local copies, waits for them, and re-layouts: 1.3 us -> 0.6 us
where the time goes in v2:
time: 39.3 us; the launch traced here: 39.2 us
  Pallas kernels  38.5 us (98%)
  local copies, waits for them, and re-layouts  0.6 us (2%)
    pallas_call x1, Pallas kernels, shards(): pl.pallas_call(functools.partial(kernel, mp_size), out_shape=pltpu.VMEM((...  38.5 us

profile of v2, /device:TPU:1, one launch (start us, length us, event | category | flops | bytes accessed | tf_op | source)
XLA Modules:
  0.0 39.2 jit_solution(494681914718003150)
XLA Ops:
  0.0 38.5 %whiten.1 = f32[1,16,64]{2,1,0:T(8,128)S(1)} custom-call(bf16[128,1024]{1,0:T(8,128)(2,1)} %tokens_hbm.1, bf16[128,3584]{1,0:T(8,128)(2,1)} %gate_hbm.1, bf16[128,3584]{1,0:T(8,128)(2,1)} %up_hbm.1, bf16[128,3584]{1,0:T(8,128)(2,1)} %hidden_grad_hbm.1, bf16[128,1024]{1,0:T(8,128)(2,1)} %out_grad_hbm.1, bf16[1024,128]{1,0:T(8,128)(2,1)} %model_hbm.1, ...), custom_call_target="tpu_custom_call" | custom-call | tf_op jit(solution)/shard_map/whiten/pallas_call | solution.py:301
  38.6 0.6 %copy.9 = f32[1,16,64]{2,1,0:T(8,128)} copy(f32[1,16,64]{2,1,0:T(8,128)S(1)} %whiten.1) | data formatting | bytes 8192

commit v3 on v2

--- a/solution.py
+++ b/solution.py
@@ -113,6 +113,7 @@
     m_sem,
     z_sem,
     f_sem,
+    far_sem,
 ):
     nx = mp_size // NC
     dp = lax.axis_index("dp")
@@ -151,16 +152,17 @@
         there = (y * mp_size + mp + apart) % plane
         return ((there // mp_size) * NZ + z, there % mp_size)
 
-    def greet_z(apart, carry):
-        pl.semaphore_signal(barrier, inc=1, device_id=z_peer(apart), device_id_type=MESH)
-        return carry
-
-    def greet_plane(apart, carry):
-        pl.semaphore_signal(barrier, inc=1, device_id=plane_peer(apart), device_id_type=MESH)
-        return carry
-
-    lax.fori_loop(1, NZ, greet_z, 0)
-    lax.fori_loop(1, plane, greet_plane, 0)
+    def along_z(semaphore, steps):
+        for apart in steps:
+            for way in (apart, NZ - apart):
+                pl.semaphore_signal(semaphore, inc=1, device_id=z_peer(way), device_id_type=MESH)
+
+    for apart in range(1, mp_size):
+        pl.semaphore_signal(barrier, inc=1, device_id=(dp, (mp + apart) % mp_size), device_id_type=MESH)
+    for apart in range(1, NY):
+        there = ((y + apart) % NY) * NZ + z
+        pl.semaphore_signal(barrier, inc=1, device_id=(there, mp), device_id_type=MESH)
+    along_z(barrier, (1, 2))
 
     weights.wait()
     upward, downward = [], []
@@ -185,14 +187,15 @@
     part[0] = jnp.where(low, inward, pltpu.roll(jnp.concatenate(upward, axis=0), RANK, 1))
     part[1] = jnp.where(low, pltpu.roll(outward, RANK, 1), jnp.concatenate(downward, axis=0))
 
-    pl.semaphore_wait(barrier, NZ - 1 + plane - 1)
+    pl.semaphore_wait(barrier, mp_size - 1 + NY - 1 + 4)
+    along_z(far_sem.at[0], (2,))
 
     sibling = (dp, x * NC + 1 - core)
     swap = pltpu.make_async_remote_copy(
         part.at[1 - core], from_core, core_sem.at[0], core_sem.at[1], device_id=sibling, device_id_type=MESH
     )
     swap.start()
-    swap.wait()
+    swap.wait_recv()
     xbuf[x] = part[core] + from_core[...]
 
     for apart in range(1, nx):
@@ -204,6 +207,8 @@
             device_id=(dp, ((x + apart) % nx) * NC + core),
             device_id_type=MESH,
         ).start()
+    pl.semaphore_wait(far_sem.at[0], 2)
+    along_z(far_sem.at[1], (4,))
     all_x = pltpu.make_async_remote_copy(
         xbuf.at[pl.ds(0, nx - 1)],
         xbuf.at[pl.ds(0, nx - 1)],
@@ -212,7 +217,6 @@
         device_id=sibling,
         device_id_type=MESH,
     )
-    all_x.wait_send()
     all_x.wait_recv()
     summed = xbuf[0]
     for i in range(1, nx):
@@ -226,7 +230,7 @@
         mbuf.at[core], mbuf.at[core], m_sem.at[0], m_sem.at[1], device_id=sibling, device_id_type=MESH
     )
     give.start()
-    give.wait()
+    give.wait_recv()
     short_low = lax.broadcasted_iota(jnp.int32, (RANK, 2 * RANK), 1) < RANK
     stacked = jnp.where(short_low, mbuf[0], mbuf[1])
 
@@ -237,6 +241,7 @@
     for i in range(mp_size):
         packed[i] = pairs[i * size : (i + 1) * size]
 
+    pl.semaphore_wait(far_sem.at[1], 2)
     for apart in sorted(range(1, NZ), key=lambda d: -min(d, NZ - d)):
         pltpu.make_async_remote_copy(
             packed.at[mp], zbuf.at[z], z_sem.at[0], z_sem.at[1], device_id=z_peer(apart), device_id_type=MESH
@@ -251,7 +256,6 @@
         device_id=sibling,
         device_id_type=MESH,
     )
-    all_z.wait_send()
     all_z.wait_recv()
     slice_sum = zbuf[0]
     for i in range(1, NZ):
@@ -274,7 +278,6 @@
         device_id=sibling,
         device_id_type=MESH,
     )
-    all_plane.wait_send()
     all_plane.wait_recv()
     for i in range(mp_size):
         piece = fbuf[i]
@@ -290,6 +293,8 @@
     turned_out = rows_out[...].T
     out_ref[0] = turned_out[RANK : RANK + 2 * RANK // mp_size, :RANK] * factor
 
+    for sent in (swap, all_x, give, all_z, all_plane):
+        sent.wait_send()
 
 def shards(tokens_in, gate_pre, up_pre, hidden_grad, out_grad, proj_model, proj_hidden):
     mp_size = lax.axis_size("mp")
@@ -329,6 +334,7 @@
             pltpu.SemaphoreType.DMA((2,)),
             pltpu.SemaphoreType.DMA((2,)),
             pltpu.SemaphoreType.DMA((2,)),
+            pltpu.SemaphoreType.REGULAR((2,)),
         ],
         compiler_params=pltpu.CompilerParams(collective_id=0, has_side_effects=True),
         name="whiten",

time: 39.3 us -> 38.2 us (0.972)
  Pallas kernels: 38.5 us -> 37.4 us
    pallas_call x1, Pallas kernels: 38.5 us -> 37.4 us  [shards(): pl.pallas_call(functools.partial(kernel, mp_size), out_shape=pltpu.VMEM((...]
where the time goes in v3:
time: 38.2 us; the launch traced here: 38.1 us
  Pallas kernels  37.4 us (98%)
  local copies, waits for them, and re-layouts  0.6 us (2%)
    pallas_call x1, Pallas kernels, shards(): pl.pallas_call(functools.partial(kernel, mp_size), out_shape=pltpu.VMEM((...  37.4 us

profile of v3, /device:TPU:1, one launch (start us, length us, event | category | flops | bytes accessed | tf_op | source)
XLA Modules:
  0.0 38.1 jit_solution(2574060686474470887)
XLA Ops:
  0.0 37.4 %whiten.1 = f32[1,16,64]{2,1,0:T(8,128)S(1)} custom-call(bf16[128,1024]{1,0:T(8,128)(2,1)} %tokens_hbm.1, bf16[128,3584]{1,0:T(8,128)(2,1)} %gate_hbm.1, bf16[128,3584]{1,0:T(8,128)(2,1)} %up_hbm.1, bf16[128,3584]{1,0:T(8,128)(2,1)} %hidden_grad_hbm.1, bf16[128,1024]{1,0:T(8,128)(2,1)} %out_grad_hbm.1, bf16[1024,128]{1,0:T(8,128)(2,1)} %model_hbm.1, ...), custom_call_target="tpu_custom_call" | custom-call | tf_op jit(solution)/shard_map/whiten/pallas_call | solution.py:306
  37.5 0.6 %copy.9 = f32[1,16,64]{2,1,0:T(8,128)} copy(f32[1,16,64]{2,1,0:T(8,128)S(1)} %whiten.1) | data formatting | bytes 8192

commit v4 on v3

--- a/solution.py
+++ b/solution.py
@@ -17,6 +17,14 @@
 BF16 = jnp.bfloat16
 MESH = pl.DeviceIdType.MESH
 NT = (((1,), (1,)), ((), ()))
+
+
+def hops(apart, size):
+    return min(apart, size - apart)
+
+
+def farthest_first(size):
+    return sorted(range(1, size), key=lambda apart: -hops(apart, size))
 
 
 def halves(value):
@@ -145,24 +153,24 @@
     barrier = pltpu.get_barrier_semaphore()
     plane = NY * mp_size
 
-    def z_peer(apart):
-        return (y * NZ + (z + apart) % NZ, mp)
-
-    def plane_peer(apart):
-        there = (y * mp_size + mp + apart) % plane
-        return ((there // mp_size) * NZ + z, there % mp_size)
-
-    def along_z(semaphore, steps):
+    def z_peer(apart, other):
+        return (y * NZ + (z + apart) % NZ, x * NC + (core + other) % NC)
+
+    def plane_peer(far_y, far_x, other):
+        return ((y + far_y) % NY) * NZ + z, ((x + far_x) % nx) * NC + (core + other) % NC
+
+    def along_z(semaphore, steps, cores):
         for apart in steps:
             for way in (apart, NZ - apart):
-                pl.semaphore_signal(semaphore, inc=1, device_id=z_peer(way), device_id_type=MESH)
+                for other in range(cores):
+                    pl.semaphore_signal(semaphore, inc=1, device_id=z_peer(way, other), device_id_type=MESH)
 
     for apart in range(1, mp_size):
         pl.semaphore_signal(barrier, inc=1, device_id=(dp, (mp + apart) % mp_size), device_id_type=MESH)
     for apart in range(1, NY):
         there = ((y + apart) % NY) * NZ + z
         pl.semaphore_signal(barrier, inc=1, device_id=(there, mp), device_id_type=MESH)
-    along_z(barrier, (1, 2))
+    along_z(barrier, (1, 2), NC)
 
     weights.wait()
     upward, downward = [], []
@@ -187,8 +195,8 @@
     part[0] = jnp.where(low, inward, pltpu.roll(jnp.concatenate(upward, axis=0), RANK, 1))
     part[1] = jnp.where(low, pltpu.roll(outward, RANK, 1), jnp.concatenate(downward, axis=0))
 
-    pl.semaphore_wait(barrier, mp_size - 1 + NY - 1 + 4)
-    along_z(far_sem.at[0], (2,))
+    pl.semaphore_wait(barrier, mp_size - 1 + NY - 1 + 4 * NC)
+    along_z(far_sem.at[0], (2,), 1)
 
     sibling = (dp, x * NC + 1 - core)
     swap = pltpu.make_async_remote_copy(
@@ -198,7 +206,7 @@
     swap.wait_recv()
     xbuf[x] = part[core] + from_core[...]
 
-    for apart in range(1, nx):
+    for apart in farthest_first(nx):
         pltpu.make_async_remote_copy(
             xbuf.at[x],
             xbuf.at[x],
@@ -208,7 +216,7 @@
             device_id_type=MESH,
         ).start()
     pl.semaphore_wait(far_sem.at[0], 2)
-    along_z(far_sem.at[1], (4,))
+    along_z(far_sem.at[1], (4,), 1)
     all_x = pltpu.make_async_remote_copy(
         xbuf.at[pl.ds(0, nx - 1)],
         xbuf.at[pl.ds(0, nx - 1)],
@@ -230,11 +238,10 @@
         mbuf.at[core], mbuf.at[core], m_sem.at[0], m_sem.at[1], device_id=sibling, device_id_type=MESH
     )
     give.start()
-    give.wait_recv()
-    short_low = lax.broadcasted_iota(jnp.int32, (RANK, 2 * RANK), 1) < RANK
-    stacked = jnp.where(short_low, mbuf[0], mbuf[1])
-
-    gram = product_6(stacked, jnp.concatenate([stacked, stacked], axis=0))
+
+    short_lane = lax.broadcasted_iota(jnp.int32, (RANK, 2 * RANK), 1)
+    block = jnp.where(short_lane // RANK == core, mbuf[core], 0.0)
+    gram = product_6(block, jnp.concatenate([block, block], axis=0))
     half_low = lax.broadcasted_iota(jnp.int32, (RANK // 2, 2 * RANK), 1) < RANK
     pairs = jnp.where(half_low, gram[: RANK // 2], gram[RANK // 2 :])
     size = packed.shape[1]
@@ -242,34 +249,50 @@
         packed[i] = pairs[i * size : (i + 1) * size]
 
     pl.semaphore_wait(far_sem.at[1], 2)
-    for apart in sorted(range(1, NZ), key=lambda d: -min(d, NZ - d)):
-        pltpu.make_async_remote_copy(
-            packed.at[mp], zbuf.at[z], z_sem.at[0], z_sem.at[1], device_id=z_peer(apart), device_id_type=MESH
-        ).start()
-    zbuf[z] = packed[mp]
-    own = pltpu.roll(stacked, (RANK + 2 * RANK - mp * (2 * RANK // mp_size)) % (2 * RANK), 1)
-    all_z = pltpu.make_async_remote_copy(
-        zbuf.at[pl.ds(0, NZ - 1)],
-        zbuf.at[pl.ds(0, NZ - 1)],
+    slot = z * NC + core
+    for apart in farthest_first(NZ):
+        for other in range(NC):
+            pltpu.make_async_remote_copy(
+                packed.at[x * NC + (core + other) % NC],
+                zbuf.at[slot],
+                z_sem.at[0],
+                z_sem.at[1],
+                device_id=z_peer(apart, other),
+                device_id_type=MESH,
+            ).start()
+    pltpu.make_async_remote_copy(
+        packed.at[x * NC + 1 - core],
+        zbuf.at[slot],
         z_sem.at[0],
         z_sem.at[1],
         device_id=sibling,
         device_id_type=MESH,
+    ).start()
+    zbuf[slot] = packed[mp]
+    give.wait_recv()
+    stacked = jnp.where(short_lane < RANK, mbuf[0], mbuf[1])
+    own = pltpu.roll(stacked, (RANK + 2 * RANK - mp * (2 * RANK // mp_size)) % (2 * RANK), 1)
+    all_z = pltpu.make_async_remote_copy(
+        zbuf.at[pl.ds(0, NC * NZ - 1)],
+        zbuf.at[pl.ds(0, NC * NZ - 1)],
+        z_sem.at[0],
+        z_sem.at[1],
+        device_id=sibling,
+        device_id_type=MESH,
     )
     all_z.wait_recv()
-    slice_sum = zbuf[0]
-    for i in range(1, NZ):
-        slice_sum = slice_sum + zbuf[i]
+    terms = [zbuf[i] for i in range(NC * NZ)]
+    while len(terms) > 1:
+        terms = [first + second for first, second in zip(terms[::2], terms[1::2])]
+    slice_sum = terms[0]
     place = y * mp_size + mp
     fbuf[place] = slice_sum
 
-    def send_plane(apart, carry):
+    others = [(i, j, k) for i in range(NY) for j in range(nx) for k in range(NC)][1:]
+    for far in sorted(others, key=lambda far: -hops(far[0], NY) - hops(far[1], nx)):
         pltpu.make_async_remote_copy(
-            fbuf.at[place], fbuf.at[place], f_sem.at[0], f_sem.at[1], device_id=plane_peer(apart), device_id_type=MESH
+            fbuf.at[place], fbuf.at[place], f_sem.at[0], f_sem.at[1], device_id=plane_peer(*far), device_id_type=MESH
         ).start()
-        return carry
-
-    lax.fori_loop(1, plane, send_plane, 0)
     all_plane = pltpu.make_async_remote_copy(
         fbuf.at[pl.ds(0, plane - 1)],
         fbuf.at[pl.ds(0, plane - 1)],
@@ -286,7 +309,7 @@
         aug[i * size : (i + 1) * size, :] = piece
     folded = aug[...]
     whole = jnp.concatenate([folded, pltpu.roll(folded, RANK, 1)], axis=0)
-    table = jnp.where(short_low, whole, own)
+    table = jnp.where(short_lane < RANK, whole, own)
 
     eliminate(table, rows_out)
     factor = math.sqrt(NY * NZ * LEN)
@@ -323,7 +346,7 @@
             pltpu.VMEM((ranks, ranks), F32),
             pltpu.VMEM((2, RANK, ranks), F32),
             pltpu.VMEM((mp_size, size, ranks), F32),
-            pltpu.VMEM((NZ, size, ranks), F32),
+            pltpu.VMEM((NC * NZ, size, ranks), F32),
             pltpu.VMEM((NY * mp_size, size, ranks), F32),
             pltpu.VMEM((RANK // 2, ranks), F32),
             pltpu.VMEM((ranks, ranks), F32),

time: 38.2 us -> 37.4 us (0.979)
  Pallas kernels: 37.4 us -> 36.7 us
    pallas_call x1, Pallas kernels: 37.4 us -> 36.7 us  [shards(): pl.pallas_call(functools.partial(kernel, mp_size), out_shape=pltpu.VMEM((...]
where the time goes in v4:
time: 37.4 us; the launch traced here: 37.3 us
  Pallas kernels  36.7 us (98%)
  local copies, waits for them, and re-layouts  0.6 us (2%)
    pallas_call x1, Pallas kernels, shards(): pl.pallas_call(functools.partial(kernel, mp_size), out_shape=pltpu.VMEM((...  36.7 us

profile of v4, /device:TPU:1, one launch (start us, length us, event | category | flops | bytes accessed | tf_op | source)
XLA Modules:
  0.0 37.3 jit_solution(9534602304641644401)
XLA Ops:
  0.0 36.7 %whiten.1 = f32[1,16,64]{2,1,0:T(8,128)S(1)} custom-call(bf16[128,1024]{1,0:T(8,128)(2,1)} %tokens_hbm.1, bf16[128,3584]{1,0:T(8,128)(2,1)} %gate_hbm.1, bf16[128,3584]{1,0:T(8,128)(2,1)} %up_hbm.1, bf16[128,3584]{1,0:T(8,128)(2,1)} %hidden_grad_hbm.1, bf16[128,1024]{1,0:T(8,128)(2,1)} %out_grad_hbm.1, bf16[1024,128]{1,0:T(8,128)(2,1)} %model_hbm.1, ...), custom_call_target="tpu_custom_call" | custom-call | tf_op jit(solution)/shard_map/whiten/pallas_call | solution.py:329
  36.7 0.6 %copy.9 = f32[1,16,64]{2,1,0:T(8,128)} copy(f32[1,16,64]{2,1,0:T(8,128)S(1)} %whiten.1) | data formatting | bytes 8192

commit v5 on v4

--- a/solution.py
+++ b/solution.py
@@ -17,6 +17,7 @@
 BF16 = jnp.bfloat16
 MESH = pl.DeviceIdType.MESH
 NT = (((1,), (1,)), ((), ()))
+TN = (((0,), (0,)), ((), ()))
 
 
 def hops(apart, size):
@@ -43,9 +44,9 @@
     lh, ll = halves(left)
     rh, rl = halves(right)
     return lax.dot_general(
-        jnp.concatenate([lh, lh, ll], axis=1),
-        jnp.concatenate([rh, rl, rh], axis=1),
-        NT,
+        jnp.concatenate([lh, lh, ll], axis=0),
+        jnp.concatenate([rh, rl, rh], axis=0),
+        TN,
         preferred_element_type=F32,
     )
 
@@ -107,7 +108,6 @@
     part,
     from_core,
     xbuf,
-    sbuf,
     mbuf,
     packed,
     zbuf,
@@ -130,7 +130,7 @@
     x, core = mp // NC, mp % NC
 
     weights = pltpu.make_async_copy(hidden_hbm, hidden, in_sem.at[0])
-    last = [
+    side = [
         pltpu.make_async_copy(model_hbm, model, in_sem.at[1]),
         pltpu.make_async_copy(tokens_hbm, tokens, in_sem.at[2]),
         pltpu.make_async_copy(out_grad_hbm, out_grad, in_sem.at[3]),
@@ -144,10 +144,8 @@
             pltpu.make_async_copy(hidden_grad_hbm.at[span, :], hidden_grad.at[span, :], block_sem.at[i, 1]),
             pltpu.make_async_copy(up_hbm.at[span, :], up.at[span, :], block_sem.at[i, 2]),
         ]
-        for copy in group:
-            copy.start()
         blocks.append(group)
-    for copy in last:
+    for copy in blocks[0] + side + blocks[1]:
         copy.start()
 
     barrier = pltpu.get_barrier_semaphore()
@@ -172,10 +170,21 @@
         pl.semaphore_signal(barrier, inc=1, device_id=(there, mp), device_id_type=MESH)
     along_z(barrier, (1, 2), NC)
 
-    weights.wait()
-    upward, downward = [], []
-    for i, group in enumerate(blocks):
-        for copy in group:
+    low = lax.broadcasted_iota(jnp.int32, (LEN // 2, 2 * RANK), 1) < RANK
+    sibling = (dp, x * NC + 1 - core)
+
+    def swap_of(kind):
+        return pltpu.make_async_remote_copy(
+            part.at[kind, 1 - core],
+            from_core.at[kind],
+            core_sem.at[kind, 0],
+            core_sem.at[kind, 1],
+            device_id=sibling,
+            device_id_type=MESH,
+        )
+
+    def project(i):
+        for copy in blocks[i]:
             copy.wait()
         for r in range(i * ROWS, (i + 1) * ROWS, 32):
             span = pl.ds(r, 32)
@@ -184,63 +193,74 @@
             lhs[0, span, :] = (hidden_grad[span, :].astype(F32) * act).astype(BF16)
             lhs[1, span, :] = (act * up[span, :].astype(F32)).astype(BF16)
         span = pl.ds(i * ROWS, ROWS)
-        upward.append(jnp.dot(lhs[0, span, :], hidden[...], preferred_element_type=F32))
-        downward.append(jnp.dot(lhs[1, span, :], hidden[...], preferred_element_type=F32))
-    for copy in last:
+        return [jnp.dot(lhs[j, span, :], hidden[...], preferred_element_type=F32) for j in range(2)]
+
+    weights.wait()
+    upward_1, downward_1 = project(0)
+    for copy in side:
         copy.wait()
     inward = jnp.dot(tokens[...], model[...], preferred_element_type=F32)
     outward = jnp.dot(out_grad[...], model[...], preferred_element_type=F32)
-    lane = lax.broadcasted_iota(jnp.int32, (LEN, 2 * RANK), 1)
-    low = lane < RANK
-    part[0] = jnp.where(low, inward, pltpu.roll(jnp.concatenate(upward, axis=0), RANK, 1))
-    part[1] = jnp.where(low, pltpu.roll(outward, RANK, 1), jnp.concatenate(downward, axis=0))
-
+    part[0, 0] = jnp.where(low, inward[: LEN // 2], pltpu.roll(inward[LEN // 2 :], RANK, 1))
+    part[0, 1] = jnp.where(low, pltpu.roll(outward[: LEN // 2], RANK, 1), outward[LEN // 2 :])
     pl.semaphore_wait(barrier, mp_size - 1 + NY - 1 + 4 * NC)
+    swap_side = swap_of(0)
+    swap_side.start()
     along_z(far_sem.at[0], (2,), 1)
-
-    sibling = (dp, x * NC + 1 - core)
-    swap = pltpu.make_async_remote_copy(
-        part.at[1 - core], from_core, core_sem.at[0], core_sem.at[1], device_id=sibling, device_id_type=MESH
-    )
-    swap.start()
-    swap.wait_recv()
-    xbuf[x] = part[core] + from_core[...]
-
-    for apart in farthest_first(nx):
-        pltpu.make_async_remote_copy(
-            xbuf.at[x],
-            xbuf.at[x],
-            x_sem.at[0],
-            x_sem.at[1],
-            device_id=(dp, ((x + apart) % nx) * NC + core),
+    upward_2, downward_2 = project(1)
+    part[1, 0] = jnp.where(low, upward_1, pltpu.roll(upward_2, RANK, 1))
+    part[1, 1] = jnp.where(low, pltpu.roll(downward_1, RANK, 1), downward_2)
+    swap_hidden = swap_of(1)
+    swap_hidden.start()
+
+    def exchange(kind, swap):
+        swap.wait_recv()
+        xbuf[kind, x] = part[kind, core] + from_core[kind]
+        for apart in farthest_first(nx):
+            pltpu.make_async_remote_copy(
+                xbuf.at[kind, x],
+                xbuf.at[kind, x],
+                x_sem.at[kind, 0],
+                x_sem.at[kind, 1],
+                device_id=(dp, ((x + apart) % nx) * NC + core),
+                device_id_type=MESH,
+            ).start()
+        return pltpu.make_async_remote_copy(
+            xbuf.at[kind, pl.ds(0, nx - 1)],
+            xbuf.at[kind, pl.ds(0, nx - 1)],
+            x_sem.at[kind, 0],
+            x_sem.at[kind, 1],
+            device_id=sibling,
             device_id_type=MESH,
-        ).start()
+        )
+
+    all_side = exchange(0, swap_side)
+    all_hidden = exchange(1, swap_hidden)
+
     pl.semaphore_wait(far_sem.at[0], 2)
     along_z(far_sem.at[1], (4,), 1)
-    all_x = pltpu.make_async_remote_copy(
-        xbuf.at[pl.ds(0, nx - 1)],
-        xbuf.at[pl.ds(0, nx - 1)],
-        x_sem.at[0],
-        x_sem.at[1],
-        device_id=sibling,
-        device_id_type=MESH,
-    )
-    all_x.wait_recv()
-    summed = xbuf[0]
+    all_side.wait_recv()
+    side_sum = xbuf[0, 0]
     for i in range(1, nx):
-        summed = summed + xbuf[i]
-
-    turned = summed.T
-    sbuf[...] = product_3(turned, turned)
-    mine = pl.ds(pl.multiple_of((1 - core) * RANK, RANK), RANK)
-    mbuf[core] = sbuf[mine, :]
+        side_sum = side_sum + xbuf[0, i]
+    all_hidden.wait_recv()
+    hidden_sum = xbuf[1, 0]
+    for i in range(1, nx):
+        hidden_sum = hidden_sum + xbuf[1, i]
+
+    left = jnp.where(core == 0, hidden_sum, side_sum)
+    right = jnp.where(core == 0, side_sum, hidden_sum)
+    both = product_3(left, right)
+    diagonal = jnp.where(low, both[:RANK], both[RANK:])
+    twice = diagonal + pltpu.roll(diagonal, RANK, 1)
+    mbuf[core] = twice
     give = pltpu.make_async_remote_copy(
         mbuf.at[core], mbuf.at[core], m_sem.at[0], m_sem.at[1], device_id=sibling, device_id_type=MESH
     )
     give.start()
 
     short_lane = lax.broadcasted_iota(jnp.int32, (RANK, 2 * RANK), 1)
-    block = jnp.where(short_lane // RANK == core, mbuf[core], 0.0)
+    block = jnp.where(low, twice, 0.0)
     gram = product_6(block, jnp.concatenate([block, block], axis=0))
     half_low = lax.broadcasted_iota(jnp.int32, (RANK // 2, 2 * RANK), 1) < RANK
     pairs = jnp.where(half_low, gram[: RANK // 2], gram[RANK // 2 :])
@@ -316,7 +336,7 @@
     turned_out = rows_out[...].T
     out_ref[0] = turned_out[RANK : RANK + 2 * RANK // mp_size, :RANK] * factor
 
-    for sent in (swap, all_x, give, all_z, all_plane):
+    for sent in (swap_side, swap_hidden, all_side, all_hidden, give, all_z, all_plane):
         sent.wait_send()
 
 def shards(tokens_in, gate_pre, up_pre, hidden_grad, out_grad, proj_model, proj_hidden):
@@ -340,10 +360,9 @@
             pltpu.VMEM((width, ranks), BF16),
             pltpu.VMEM((units, ranks), BF16),
             pltpu.VMEM((2, length, units), BF16),
-            pltpu.VMEM((2, length, ranks), F32),
-            pltpu.VMEM((length, ranks), F32),
-            pltpu.VMEM((mp_size // NC, length, ranks), F32),
-            pltpu.VMEM((ranks, ranks), F32),
+            pltpu.VMEM((2, NC, length // 2, ranks), F32),
+            pltpu.VMEM((2, length // 2, ranks), F32),
+            pltpu.VMEM((2, mp_size // NC, length // 2, ranks), F32),
             pltpu.VMEM((2, RANK, ranks), F32),
             pltpu.VMEM((mp_size, size, ranks), F32),
             pltpu.VMEM((NC * NZ, size, ranks), F32),
@@ -352,8 +371,8 @@
             pltpu.VMEM((ranks, ranks), F32),
             pltpu.SemaphoreType.DMA((4,)),
             pltpu.SemaphoreType.DMA((LEN // ROWS, 3)),
-            pltpu.SemaphoreType.DMA((2,)),
-            pltpu.SemaphoreType.DMA((2,)),
+            pltpu.SemaphoreType.DMA((2, 2)),
+            pltpu.SemaphoreType.DMA((2, 2)),
             pltpu.SemaphoreType.DMA((2,)),
             pltpu.SemaphoreType.DMA((2,)),
             pltpu.SemaphoreType.DMA((2,)),

time: 37.4 us -> 36.6 us (0.979)
  Pallas kernels: 36.7 us -> 35.9 us
    pallas_call x1, Pallas kernels: 36.7 us -> 35.9 us  [shards(): pl.pallas_call(functools.partial(kernel, mp_size), out_shape=pltpu.VMEM((...]
where the time goes in v5:
time: 36.6 us; the launch traced here: 36.5 us
  Pallas kernels  35.9 us (98%)
  local copies, waits for them, and re-layouts  0.6 us (2%)
    pallas_call x1, Pallas kernels, shards(): pl.pallas_call(functools.partial(kernel, mp_size), out_shape=pltpu.VMEM((...  35.9 us

profile of v5, /device:TPU:1, one launch (start us, length us, event | category | flops | bytes accessed | tf_op | source)
XLA Modules:
  0.0 36.5 jit_solution(13471152225142251141)
XLA Ops:
  0.0 35.9 %whiten.1 = f32[1,16,64]{2,1,0:T(8,128)S(1)} custom-call(bf16[128,1024]{1,0:T(8,128)(2,1)} %tokens_hbm.1, bf16[128,3584]{1,0:T(8,128)(2,1)} %gate_hbm.1, bf16[128,3584]{1,0:T(8,128)(2,1)} %up_hbm.1, bf16[128,3584]{1,0:T(8,128)(2,1)} %hidden_grad_hbm.1, bf16[128,1024]{1,0:T(8,128)(2,1)} %out_grad_hbm.1, bf16[1024,128]{1,0:T(8,128)(2,1)} %model_hbm.1, ...), custom_call_target="tpu_custom_call" | custom-call | tf_op jit(solution)/shard_map/whiten/pallas_call | solution.py:349
  35.9 0.6 %copy.9 = f32[1,16,64]{2,1,0:T(8,128)} copy(f32[1,16,64]{2,1,0:T(8,128)S(1)} %whiten.1) | data formatting | bytes 8192

commit v6 on v5

--- a/solution.py
+++ b/solution.py
@@ -183,7 +183,7 @@
             device_id_type=MESH,
         )
 
-    def project(i):
+    def weigh(i):
         for copy in blocks[i]:
             copy.wait()
         for r in range(i * ROWS, (i + 1) * ROWS, 32):
@@ -192,26 +192,9 @@
             act = half + half * jnp.tanh(half)
             lhs[0, span, :] = (hidden_grad[span, :].astype(F32) * act).astype(BF16)
             lhs[1, span, :] = (act * up[span, :].astype(F32)).astype(BF16)
-        span = pl.ds(i * ROWS, ROWS)
-        return [jnp.dot(lhs[j, span, :], hidden[...], preferred_element_type=F32) for j in range(2)]
-
-    weights.wait()
-    upward_1, downward_1 = project(0)
-    for copy in side:
-        copy.wait()
-    inward = jnp.dot(tokens[...], model[...], preferred_element_type=F32)
-    outward = jnp.dot(out_grad[...], model[...], preferred_element_type=F32)
-    part[0, 0] = jnp.where(low, inward[: LEN // 2], pltpu.roll(inward[LEN // 2 :], RANK, 1))
-    part[0, 1] = jnp.where(low, pltpu.roll(outward[: LEN // 2], RANK, 1), outward[LEN // 2 :])
-    pl.semaphore_wait(barrier, mp_size - 1 + NY - 1 + 4 * NC)
-    swap_side = swap_of(0)
-    swap_side.start()
-    along_z(far_sem.at[0], (2,), 1)
-    upward_2, downward_2 = project(1)
-    part[1, 0] = jnp.where(low, upward_1, pltpu.roll(upward_2, RANK, 1))
-    part[1, 1] = jnp.where(low, pltpu.roll(downward_1, RANK, 1), downward_2)
-    swap_hidden = swap_of(1)
-    swap_hidden.start()
+
+    def project(i, j):
+        return jnp.dot(lhs[j, pl.ds(i * ROWS, ROWS), :], hidden[...], preferred_element_type=F32)
 
     def exchange(kind, swap):
         swap.wait_recv()
@@ -234,7 +217,28 @@
             device_id_type=MESH,
         )
 
+    weights.wait()
+    weigh(0)
+    upward_1, downward_1 = project(0, 0), project(0, 1)
+    for copy in side:
+        copy.wait()
+    inward = jnp.dot(tokens[...], model[...], preferred_element_type=F32)
+    outward = jnp.dot(out_grad[...], model[...], preferred_element_type=F32)
+    part[0, 0] = jnp.where(low, inward[: LEN // 2], pltpu.roll(inward[LEN // 2 :], RANK, 1))
+    part[0, 1] = jnp.where(low, pltpu.roll(outward[: LEN // 2], RANK, 1), outward[LEN // 2 :])
+    pl.semaphore_wait(barrier, mp_size - 1 + NY - 1 + 4 * NC)
+    swap_side = swap_of(0)
+    swap_side.start()
+    along_z(far_sem.at[0], (2,), 1)
+    weigh(1)
+    upward_2 = project(1, 0)
     all_side = exchange(0, swap_side)
+    downward_2 = project(1, 1)
+    part[1, 0] = jnp.where(low, upward_1, pltpu.roll(upward_2, RANK, 1))
+    part[1, 1] = jnp.where(low, pltpu.roll(downward_1, RANK, 1), downward_2)
+    swap_hidden = swap_of(1)
+    swap_hidden.start()
+
     all_hidden = exchange(1, swap_hidden)
 
     pl.semaphore_wait(far_sem.at[0], 2)

time: 36.6 us -> 36.4 us (level)
  no operation moved by 1% of the time
where the time goes in v6:
time: 36.4 us; the launch traced here: 36.3 us
  Pallas kernels  35.7 us (98%)
  local copies, waits for them, and re-layouts  0.6 us (2%)
    pallas_call x1, Pallas kernels, shards(): pl.pallas_call(functools.partial(kernel, mp_size), out_shape=pltpu.VMEM((...  35.7 us

profile of v6, /device:TPU:1, one launch (start us, length us, event | category | flops | bytes accessed | tf_op | source)
XLA Modules:
  0.0 36.3 jit_solution(5306715759923943353)
XLA Ops:
  0.0 35.7 %whiten.1 = f32[1,16,64]{2,1,0:T(8,128)S(1)} custom-call(bf16[128,1024]{1,0:T(8,128)(2,1)} %tokens_hbm.1, bf16[128,3584]{1,0:T(8,128)(2,1)} %gate_hbm.1, bf16[128,3584]{1,0:T(8,128)(2,1)} %up_hbm.1, bf16[128,3584]{1,0:T(8,128)(2,1)} %hidden_grad_hbm.1, bf16[128,1024]{1,0:T(8,128)(2,1)} %out_grad_hbm.1, bf16[1024,128]{1,0:T(8,128)(2,1)} %model_hbm.1, ...), custom_call_target="tpu_custom_call" | custom-call | tf_op jit(solution)/shard_map/whiten/pallas_call | solution.py:353
  35.7 0.6 %copy.9 = f32[1,16,64]{2,1,0:T(8,128)} copy(f32[1,16,64]{2,1,0:T(8,128)S(1)} %whiten.1) | data formatting | bytes 8192
